TPU v7x, 128 devices: a whole 4x4x4 slice. The times are simulated.
128 devices in a mesh: rep: 4 (over x_hi, core), shard: 32 (over y, x_lo, z).
Axes of the slice: x: 4 (x_hi: 2, x_lo: 2; x = x_hi * 2 + x_lo), y: 4, z: 4, core: 2. Of those that a mesh axis runs over, the one named last changes fastest.
Arguments:
- inputs: bfloat16 [128, 128, 1024], P(('rep', 'shard')), may hold values from -6 to 6
- lengths: int32 [128], P(('rep', 'shard')), may hold values from 32 to 128, as said below
- cotangent: bfloat16 [128, 128, 1024], P(('rep', 'shard')), may hold values from -6 to 6
- w_qkv: bfloat16 [1, 1024, 3072], P(None, 'shard'), may hold values from -0.1875 to 0.1875
- b_qv: bfloat16 [1, 2, 1024], P(None, None, 'shard'), may hold values from -4 to 4
- w_att: bfloat16 [1, 1024, 1024], P(None, 'shard'), may hold values from -1 to 1
- b_att: bfloat16 [1, 1024], P(None, 'shard'), may hold values from -4 to 4
- norm1_gain: bfloat16 [1, 1024], P(None, 'shard'), may hold values from 0.5 to 1.5
- norm1_bias: bfloat16 [1, 1024], P(None, 'shard'), may hold values from -4 to 4
- w_in: bfloat16 [1, 1024, 4096], P(None, 'shard'), may hold values from -0.1875 to 0.1875
- b_in: bfloat16 [1, 4096], P(None, 'shard'), may hold values from -4 to 4
- w_out: bfloat16 [1, 4096, 1024], P(None, 'shard'), may hold values from -0.09375 to 0.09375
- b_out: bfloat16 [1, 1024], P(None, 'shard'), may hold values from -4 to 4
- norm2_gain: bfloat16 [1, 1024], P(None, 'shard'), may hold values from 0.5 to 1.5
- norm2_bias: bfloat16 [1, 1024], P(None, 'shard'), may hold values from -4 to 4
Outputs:
- outputs: bfloat16 [128, 128, 1024], P(('rep', 'shard'))
- grad_inputs: float32 [128, 128, 1024], P(('rep', 'shard'))
- grad_w_qkv: float32 [1, 1024, 3072], P(None, 'shard')
- grad_b_qv: float32 [1, 2, 1024], P(None, None, 'shard')
- grad_w_att: float32 [1, 1024, 1024], P(None, 'shard')
- grad_b_att: float32 [1, 1024], P(None, 'shard')
- grad_norm1_gain: float32 [1, 1024], P(None, 'shard')
- grad_norm1_bias: float32 [1, 1024], P(None, 'shard')
- grad_w_in: float32 [1, 1024, 4096], P(None, 'shard')
- grad_b_in: float32 [1, 4096], P(None, 'shard')
- grad_w_out: float32 [1, 4096, 1024], P(None, 'shard')
- grad_b_out: float32 [1, 1024], P(None, 'shard')
- grad_norm2_gain: float32 [1, 1024], P(None, 'shard')
- grad_norm2_bias: float32 [1, 1024], P(None, 'shard')
Inputs may be any that keep to these rules, and one draw needn't show every extreme that they name: `lengths`: some sequence has all 128 positions valid.
All inputs are finite; a program needn't handle non-finite values.
Results may differ from a plain program's by a relative error of at most 0.013.
Values may be sent and summed in bfloat16 or wider, within the bound.
No kernel may reach another device: no remote copies, remote signals or barrier semaphores. Data moves between devices by JAX's collectives and lax.ppermute only.
A program may use at most 192 MiB of HBM per device.

v0:
```python
import math
import jax
import jax.numpy as jnp
from jax import lax
from jax.sharding import PartitionSpec as P

HEAD_DIM = 64
LAYERS = 1
EPS = 1e-12
ROOT_HALF = 0.7071067811865476
INV_ROOT_TWO_PI = 0.3989422804014327


def sent_together(arrays, axis, dim, along):
    columns = [a.reshape(*a.shape[:along], -1) for a in arrays]
    both = jnp.concatenate(columns, axis=along)
    filled, at, done = (lax.all_gather(both, axis, axis=dim, tiled=True), 0, [])
    for a, column in zip(arrays, columns):
        share = filled[..., at : at + column.shape[along]]
        done.append(share.reshape(*share.shape[:along], *a.shape[along:]))
        at += column.shape[along]
    return tuple(done)


def in_one_piece(arrays, axis, dim, along):
    columns = [a.reshape(*a.shape[:along], -1) for a in arrays]
    both = jnp.concatenate(columns, axis=along)
    filled, at, done = (lax.psum_scatter(both, axis, scatter_dimension=dim, tiled=True), 0, [])
    for a, column in zip(arrays, columns):
        share = filled[..., at : at + column.shape[along]]
        done.append(share.reshape(*share.shape[:along], *a.shape[along:]))
        at += column.shape[along]
    return tuple(done)


def together(arrays, axis):
    line, at, done = (jnp.concatenate([a.reshape(-1) for a in arrays]), 0, [])
    so_far = lax.psum(line, axis)
    for a in arrays:
        done.append(so_far[at : at + a.size].reshape(a.shape))
        at += a.size
    return tuple(done)


def batched(form, left, right):
    return jnp.einsum(form, left, right, preferred_element_type=jnp.float32)


def layer_norm(residual, gain, shift):
    row_mean = jnp.mean(residual, axis=-1, keepdims=True)
    centered = residual - row_mean
    variance = jnp.mean(centered * centered, axis=-1, keepdims=True)
    inv_std = lax.rsqrt(variance + EPS)
    normed = centered * inv_std
    return (normed * gain.astype(jnp.float32) + shift.astype(jnp.float32), normed, inv_std)


def norm_backward(upstream, normed, inv_std, gain):
    grad_gain = jnp.sum(upstream * normed, axis=0)
    grad_shift = jnp.sum(upstream, axis=0)
    scaled = upstream * gain.astype(jnp.float32)
    grad_res = inv_std * (
        scaled
        - jnp.mean(scaled, axis=-1, keepdims=True)
        - normed * jnp.mean(scaled * normed, axis=-1, keepdims=True)
    )
    return (grad_res, grad_gain, grad_shift)


def attention_scores(query_bf, key_bf, key_valid):
    scores = batched("bqhe,bkhe->bhqk", query_bf, key_bf) * (1.0 / math.sqrt(HEAD_DIM))
    return jnp.where(key_valid[:, None, None, :], scores, -1e30)


def layer_forward(hidden, hidden_bf, params, key_valid, batch_size):
    (
        w_qkv,
        b_qv,
        w_att,
        b_att,
        gain_one,
        shift_one,
        w_in,
        b_in,
        w_out,
        b_out,
        gain_two,
        shift_two,
    ) = params
    model_width = hidden.shape[1]
    seq_count = hidden.shape[0] // batch_size
    shape_heads = (batch_size, seq_count, model_width // HEAD_DIM, HEAD_DIM)
    packed = jnp.dot(hidden_bf, w_qkv, preferred_element_type=jnp.float32)
    bias_qv = b_qv.astype(jnp.float32)
    query_bf = (packed[:, :model_width] + bias_qv[0]).astype(jnp.bfloat16).reshape(shape_heads)
    key_bf = packed[:, model_width : 2 * model_width].astype(jnp.bfloat16).reshape(shape_heads)
    value_bf = (packed[:, 2 * model_width :] + bias_qv[1]).astype(jnp.bfloat16).reshape(shape_heads)
    scores = attention_scores(query_bf, key_bf, key_valid)
    row_max = jnp.max(scores, axis=-1, keepdims=True)
    row_lse = row_max + jnp.log(jnp.sum(jnp.exp(scores - row_max), axis=-1, keepdims=True))
    probs_bf = jnp.exp(scores - row_lse).astype(jnp.bfloat16)
    context_bf = (
        batched("bhqk,bkhe->bqhe", probs_bf, value_bf).astype(jnp.bfloat16).reshape(-1, model_width)
    )
    first = (
        hidden
        + jnp.dot(context_bf, w_att, preferred_element_type=jnp.float32)
        + b_att.astype(jnp.float32)
    )
    middle, normed_one, inv_one = layer_norm(first, gain_one, shift_one)
    middle_bf = middle.astype(jnp.bfloat16)
    pre_act = jnp.dot(middle_bf, w_in, preferred_element_type=jnp.float32) + b_in.astype(
        jnp.float32
    )
    act_bf = (pre_act * 0.5 * (1.0 + jax.scipy.special.erf(pre_act * ROOT_HALF))).astype(
        jnp.bfloat16
    )
    second = (
        middle
        + jnp.dot(act_bf, w_out, preferred_element_type=jnp.float32)
        + b_out.astype(jnp.float32)
    )
    result, normed_two, inv_two = layer_norm(second, gain_two, shift_two)
    stored = (
        hidden_bf,
        query_bf,
        key_bf,
        value_bf,
        row_lse,
        context_bf,
        normed_one,
        inv_one,
        middle_bf,
        pre_act,
        act_bf,
        normed_two,
        inv_two,
    )
    return (result, stored)


def layer_backward(upstream, stored, params, key_valid):
    (
        w_qkv,
        b_qv,
        w_att,
        b_att,
        gain_one,
        shift_one,
        w_in,
        b_in,
        w_out,
        b_out,
        gain_two,
        shift_two,
    ) = params
    (
        hidden_bf,
        query_bf,
        key_bf,
        value_bf,
        row_lse,
        context_bf,
        normed_one,
        inv_one,
        middle_bf,
        pre_act,
        act_bf,
        normed_two,
        inv_two,
    ) = stored
    model_width = upstream.shape[1]
    shape_heads = query_bf.shape
    grad_second, grad_gain_two, grad_shift_two = norm_backward(
        upstream, normed_two, inv_two, gain_two
    )
    grad_b_out = jnp.sum(grad_second, axis=0)
    second_bf = grad_second.astype(jnp.bfloat16)
    grad_w_out = jnp.dot(act_bf.T, second_bf, preferred_element_type=jnp.float32)
    back_act = jnp.dot(second_bf, w_out.T, preferred_element_type=jnp.float32)
    cumulative = 0.5 * (1.0 + jax.scipy.special.erf(pre_act * ROOT_HALF))
    density = jnp.exp(-0.5 * pre_act * pre_act) * INV_ROOT_TWO_PI
    grad_pre = back_act * (cumulative + pre_act * density)
    pre_bf = grad_pre.astype(jnp.bfloat16)
    grad_w_in = jnp.dot(middle_bf.T, pre_bf, preferred_element_type=jnp.float32)
    grad_b_in = jnp.sum(grad_pre, axis=0)
    grad_middle = grad_second + jnp.dot(pre_bf, w_in.T, preferred_element_type=jnp.float32)
    grad_first, grad_gain_one, grad_shift_one = norm_backward(
        grad_middle, normed_one, inv_one, gain_one
    )
    grad_b_att = jnp.sum(grad_first, axis=0)
    first_bf = grad_first.astype(jnp.bfloat16)
    grad_w_att = jnp.dot(context_bf.T, first_bf, preferred_element_type=jnp.float32)
    grad_context = (
        jnp.dot(first_bf, w_att.T, preferred_element_type=jnp.float32)
        .astype(jnp.bfloat16)
        .reshape(shape_heads)
    )
    scores = attention_scores(query_bf, key_bf, key_valid)
    probs = jnp.exp(scores - row_lse)
    grad_value = batched("bhqk,bqhe->bkhe", probs.astype(jnp.bfloat16), grad_context).reshape(
        -1, model_width
    )
    grad_probs = batched("bqhe,bkhe->bhqk", grad_context, value_bf)
    inner = jnp.sum(probs * grad_probs, axis=-1, keepdims=True)
    grad_scores = (probs * (grad_probs - inner) * (1.0 / math.sqrt(HEAD_DIM))).astype(jnp.bfloat16)
    grad_query = batched("bhqk,bkhe->bqhe", grad_scores, key_bf).reshape(-1, model_width)
    grad_key = batched("bhqk,bqhe->bkhe", grad_scores, query_bf).reshape(-1, model_width)
    grad_b_qv = jnp.stack([jnp.sum(grad_query, axis=0), jnp.sum(grad_value, axis=0)])
    packed_bf = jnp.concatenate([grad_query, grad_key, grad_value], axis=1).astype(jnp.bfloat16)
    grad_w_qkv = jnp.dot(hidden_bf.T, packed_bf, preferred_element_type=jnp.float32)
    grad_hidden = grad_first + jnp.dot(packed_bf, w_qkv.T, preferred_element_type=jnp.float32)
    terms = (
        grad_w_qkv,
        grad_b_qv,
        grad_w_att,
        grad_b_att,
        grad_gain_one,
        grad_shift_one,
        grad_w_in,
        grad_b_in,
        grad_w_out,
        grad_b_out,
        grad_gain_two,
        grad_shift_two,
    )
    return (grad_hidden, terms)


def body(
    inputs,
    lengths,
    cotangent,
    w_qkv,
    b_qv,
    w_att,
    b_att,
    norm1_gain,
    norm1_bias,
    w_in,
    b_in,
    w_out,
    b_out,
    norm2_gain,
    norm2_bias,
):
    batch_size, seq_count, model_width = inputs.shape
    key_valid = lax.broadcasted_iota(jnp.int32, (batch_size, seq_count), 1) < lengths[:, None]
    hidden = inputs.astype(jnp.float32).reshape(-1, model_width)
    hidden_bf = inputs.reshape(-1, model_width)
    kept_params = []
    layer_index = 0
    params = (
        lax.all_gather(w_qkv[layer_index], "shard", axis=0, tiled=True),
        lax.all_gather(b_qv[layer_index], "shard", axis=1, tiled=True),
        *sent_together(
            (
                w_att[layer_index],
                b_att[layer_index],
                norm1_gain[layer_index],
                norm1_bias[layer_index],
                w_in[layer_index],
            ),
            "shard",
            0,
            1,
        ),
        *sent_together((b_in[layer_index], w_out[layer_index]), "shard", 0, 1),
        lax.all_gather(b_out[layer_index], "shard", axis=0, tiled=True),
        lax.all_gather(norm2_gain[layer_index], "shard", axis=0, tiled=True),
        lax.all_gather(norm2_bias[layer_index], "shard", axis=0, tiled=True),
    )
    hidden, stored = layer_forward(hidden, hidden_bf, params, key_valid, batch_size)
    hidden_bf = hidden.astype(jnp.bfloat16)
    kept_params.append(params)
    stored_list = [stored]
    outputs = hidden_bf.reshape(inputs.shape)
    upstream = cotangent.astype(jnp.float32).reshape(-1, model_width)
    owned = [None] * LAYERS
    for layer_index in reversed(range(LAYERS)):
        params = (
            lax.all_gather(w_qkv[layer_index], "shard", axis=0, tiled=True),
            lax.all_gather(b_qv[layer_index], "shard", axis=1, tiled=True),
            *sent_together(
                (
                    w_att[layer_index],
                    b_att[layer_index],
                    norm1_gain[layer_index],
                    norm1_bias[layer_index],
                    w_in[layer_index],
                ),
                "shard",
                0,
                1,
            ),
            *sent_together((b_in[layer_index], w_out[layer_index]), "shard", 0, 1),
            lax.all_gather(b_out[layer_index], "shard", axis=0, tiled=True),
            lax.all_gather(norm2_gain[layer_index], "shard", axis=0, tiled=True),
            lax.all_gather(norm2_bias[layer_index], "shard", axis=0, tiled=True),
        )
        upstream, terms = layer_backward(upstream, stored_list[layer_index], params, key_valid)
        shares = (
            lax.psum_scatter(terms[0], "shard", scatter_dimension=0, tiled=True),
            lax.psum_scatter(terms[1], "shard", scatter_dimension=1, tiled=True),
            *in_one_piece((terms[2], terms[3], terms[4], terms[5], terms[6]), "shard", 0, 1),
            *in_one_piece((terms[7], terms[8]), "shard", 0, 1),
            lax.psum_scatter(terms[9], "shard", scatter_dimension=0, tiled=True),
            lax.psum_scatter(terms[10], "shard", scatter_dimension=0, tiled=True),
            lax.psum_scatter(terms[11], "shard", scatter_dimension=0, tiled=True),
        )
        shares = together(
            (
                shares[0],
                shares[1],
                shares[2],
                shares[3],
                shares[4],
                shares[5],
                shares[6],
                shares[7],
                shares[8],
                shares[9],
                shares[10],
                shares[11],
            ),
            "rep",
        )
        owned[layer_index] = shares
    final = [jnp.stack([owned[0][member]]) for member in range(12)]
    grad_inputs = upstream.reshape(inputs.shape)
    return (
        outputs,
        grad_inputs,
        final[0],
        final[1],
        final[2],
        final[3],
        final[4],
        final[5],
        final[6],
        final[7],
        final[8],
        final[9],
        final[10],
        final[11],
    )


def solution(mesh):
    return jax.shard_map(
        body,
        mesh=mesh,
        in_specs=(
            P(("rep", "shard"), None, None),
            P(("rep", "shard")),
            P(("rep", "shard"), None, None),
            P(None, "shard", None),
            P(None, None, "shard"),
            P(None, "shard", None),
            P(None, "shard"),
            P(None, "shard"),
            P(None, "shard"),
            P(None, "shard", None),
            P(None, "shard"),
            P(None, "shard", None),
            P(None, "shard"),
            P(None, "shard"),
            P(None, "shard"),
        ),
        out_specs=(
            P(("rep", "shard"), None, None),
            P(("rep", "shard"), None, None),
            P(None, "shard", None),
            P(None, None, "shard"),
            P(None, "shard", None),
            P(None, "shard"),
            P(None, "shard"),
            P(None, "shard"),
            P(None, "shard", None),
            P(None, "shard"),
            P(None, "shard", None),
            P(None, "shard"),
            P(None, "shard"),
            P(None, "shard"),
        ),
        check_vma=False,
    )
```

profile of v0, /device:TPU:1, one launch (start us, length us, event | category | flops | bytes accessed | tf_op | source)
XLA Modules:
  0.0 1430.6 jit_solution(17285094910690135515)
XLA Ops:
  8.0 0.8 copy.91
  8.8 1.8 pad_maximum_fusion.4
  12.9 2.0 concatenate.21
  17.6 74.4 %all-reduce.7 = (bf16[1024]{0:T(1024)(128)(2,1)S(1)}, bf16[1024]{0:T(1024)(128)(2,1)S(1)}, bf16[1024]{0:T(1024)(128)(2,1)S(1)}) all-reduce(bf16[1024]{0:T(1024)(128)(2,1)S(1)} %dynamic-update-slice, bf16[1024]{0:T(1024)(128)(2,1)S(1)} %dynamic-update-slice.2, ...), channel_id=4, replica_groups=mesh['rep'=4,'shard'=32] {'shard'}, use_global_device_ids=true, to_apply=%add | all-reduce | flops 3072 | bytes 12288
  92.2 68.2 %all-gather.1 = bf16[1,2,1024]{1,0,2:T(2,128)(2,1)S(1)} all-gather(bf16[1,2,32]{1,0,2:T(2,128)(2,1)S(1)} %copy.83), channel_id=3, replica_groups=mesh['rep'=4,'shard'=32] {'shard'}, dimensions={2}, use_global_device_ids=true | all-gather | bytes 4224 | tf_op jit(solution)/shard_map/all_gather | solution.py:255
  161.0 7.2 slice_reduce_fusion
  168.2 3.8 fusion.11
  173.6 156.3 %all-gather.11.cloned.1.call-done = bf16[4096,1025]{1,0:T(8,128)(2,1)} async-done(((bf16[128,1025]{1,0:T(8,128)(2,1)}), bf16[4096,1025]{1,0:T(8,128)(2,1)}) %all-gather.11.cloned.1.call-update) | async-done | bytes 8396816 | tf_op jit(solution)/shard_map/all_gather | solution.py:17
  329.9 1.6 convert_reduce_fusion
  331.5 174.2 %all-gather.9.cloned.1.call-done = bf16[1024,5123]{1,0:T(8,128)(2,1)} async-done(((bf16[32,5123]{1,0:T(8,128)(2,1)}), bf16[1024,5123]{1,0:T(8,128)(2,1)}) %all-gather.9.cloned.1.call-update) | async-done | bytes 10491920 | tf_op jit(solution)/shard_map/all_gather | solution.py:17
  505.7 1.6 convert_reduce_fusion.3
  507.3 2.1 fusion.110
  509.7 6.9 fusion.13
  516.7 3.2 fusion.111
  520.5 1.0 fusion.102
  521.4 4.3 fusion.114
  525.8 3.7 multiply_reduce_fusion.1
  529.8 0.8 fusion.53
  531.3 1.3 fusion.115
  532.7 2.1 convolution_convert_fusion
  534.8 2.3 fusion.106
  537.2 1.0 copy.109
  538.5 6.4 convolution_bitcast_fusion
  544.9 12.6 copy.107
  557.6 1.0 copy-done.6
  558.5 4.0 fusion.91
  562.5 6.4 pad_maximum_fusion
  569.9 2.7 fusion.88
  572.5 8.3 fusion.73
  580.8 25.0 %concatenate.24 = f32[1024,5123]{1,0:T(8,128)} concatenate(f32[1024,1024]{1,0:T(8,128)} %fusion.88, f32[1024,1]{1,0:T(8,128)S(1)} %copy.98, f32[1024,1]{1,0:T(8,128)S(1)} %copy.99, f32[1024,1]{1,0:T(8,128)S(1)} %copy.100, f32[1024,4096]{1,0:T(8,128)} %fusion.73), dimensions={1} | concatenate | bytes 41967616 | tf_op jit(solution)/shard_map/concatenate | solution.py:27
  606.6 131.1 %all-reduce.6 = (f32[1024]{0:T(1024)S(1)}, f32[1024]{0:T(1024)S(1)}, f32[1024]{0:T(1024)S(1)}) all-reduce(f32[1024]{0:T(1024)S(1)} %get-tuple-element.35, f32[1024]{0:T(1024)S(1)} %get-tuple-element.19, f32[1024]{0:T(1024)S(1)} %convert_reduce_fusion.1), channel_id=11, replica_groups=mesh['rep'=4,'shard'=32] {'shard'}, use_global_device_ids=true, to_apply=%region_22.23.clone | all-reduce | flops 3072 | bytes 24576
  738.0 0.8 copy.110
  738.8 143.8 %reduce-scatter.13.cloned.1.call-done = f32[32,3072]{1,0:T(8,128)} async-done(((f32[1024,3072]{1,0:T(8,128)}), f32[32,3072]{1,0:T(8,128)}) %reduce-scatter.13.cloned.1.call-update) | async-done | bytes 393232 | tf_op jit(solution)/shard_map/reduce_scatter | solution.py:303
  882.6 1.1 copy.111
  883.7 205.5 %reduce-scatter.11.cloned.1.call-done = f32[128,1025]{0,1:T(8,128)} async-done(((f32[4096,1025]{0,1:T(8,128)}), f32[128,1025]{0,1:T(8,128)}) %reduce-scatter.11.cloned.1.call-update) | async-done | bytes 524816 | tf_op jit(solution)/shard_map/reduce_scatter | solution.py:28
  1089.2 1.1 slice.157
  1091.2 255.8 %reduce-scatter.9.cloned.1.call-done = f32[32,5123]{1,0:T(8,128)} async-done(((f32[1024,5123]{1,0:T(8,128)}), f32[32,5123]{1,0:T(8,128)}) %reduce-scatter.9.cloned.1.call-update) | async-done | bytes 655760 | tf_op jit(solution)/shard_map/reduce_scatter | solution.py:28
  1347.0 1.2 slice_bitcast_fusion
  1348.4 0.9 slice_bitcast_fusion.1
  1349.3 1.1 slice_reduce_fusion.2
  1350.4 16.6 %concatenate.26 = f32[393600]{0:T(1024)} concatenate(f32[98304]{0:T(1024)S(1)} %bitcast.137, f32[64]{0:T(128)S(1)} %reshape.292, f32[32768]{0:T(1024)S(1)} %bitcast.148, f32[32]{0:T(128)S(1)} %get-tuple-element.23, f32[32]{0:T(128)S(1)} %get-tuple-element.22, f32[32]{0:T(128)S(1)} %get-tuple-element.21, f32[131072]{0:T(1024)S(1)} %bitcast.136, f32[128]{0:T(128)S(1)} %slice_bitcast_fusion.9, ...), dimensions={0} | concatenate | bytes 3148800 | tf_op jit(solution)/shard_map/concatenate | solution.py:37
  1367.1 5.8 fusion.50
  1372.9 42.4 %all-reduce.10.cloned.1.call-done = f32[393600]{0:T(1024)} async-done(((f32[393600]{0:T(1024)}), f32[393600]{0:T(1024)}) %all-reduce.10.cloned.1.call-update) | async-done | bytes 1574416 | tf_op jit(solution)/shard_map/psum | solution.py:38
  1416.6 1.0 slice.160
  1418.3 1.5 fusion.105
  1419.8 0.9 stack_reshape.19
  1420.7 0.8 stack_reshape.15
  1421.5 0.9 stack_reshape.18
  (129 shorter events, 14.4 us)
Async XLA Ops:
  7.2 8.5 copy-start.17
  7.2 9.7 copy-start.19
  7.2 10.0 copy-start.20
  7.2 10.2 copy-start.21
  7.2 84.9 %copy-start.18 = (bf16[1,2,32]{2,1,0:T(2,128)(2,1)S(1)}, bf16[1,2,32]{2,1,0:T(2,128)(2,1)}, u32[]{:S(2)}) copy-start(bf16[1,2,32]{2,1,0:T(2,128)(2,1)} %param.19) | copy-start | bytes 388
  7.2 161.0 %all-gather.13.cloned.1.call-start = ((), (), s32[]{:S(2)}) async-start(), calls=%async_computation.9 | async-start | bytes 6488064 | tf_op jit(solution)/shard_map/all_gather | solution.py:254
  8.0 321.9 %all-gather.11.cloned.1.call-start = ((), (), s32[]{:S(2)}) async-start(), calls=%async_computation.5 | async-start | bytes 9732096 | tf_op jit(solution)/shard_map/all_gather | solution.py:17
  10.6 157.6 %copy-start = (bf16[1,128,1024]{2,1,0:T(8,128)(2,1)S(1)}, bf16[1,128,1024]{2,1,0:T(8,128)(2,1)}, u32[]{:S(2)}) copy-start(bf16[1,128,1024]{2,1,0:T(8,128)(2,1)} %param.15) | copy-start | bytes 786436
  10.6 495.1 %all-gather.9.cloned.1.call-start = ((), (), s32[]{:S(2)}) async-start(), calls=%async_computation.4 | async-start | bytes 11083776 | tf_op jit(solution)/shard_map/all_gather | solution.py:17
  14.9 723.0 %reduce-scatter.15.cloned.1.call-start = ((), (), s32[]{:S(2)}) async-start(), calls=%async_computation.11 | async-start | bytes 540672
  172.3 1.2 copy-start.15
  172.5 1.0 copy-start.14
  173.6 335.9 %copy-start.3 = (bf16[16,64,128]{2,1,0:T(8,128)(2,1)}, bf16[16,64,128]{2,1,0:T(8,128)(2,1)S(1)}, u32[]{:S(2)}) copy-start(bf16[16,64,128]{2,1,0:T(8,128)(2,1)S(1)} %convolution_convert_fusion.1) | copy-start | bytes 786436
  509.7 7.0 copy-start.16
  516.7 4.8 copy-start.1
  516.7 3.5 copy-start.2
  520.5 5.3 slice-start.1
  521.4 4.4 copy-start.5
  521.4 4.4 slice-start.2
  521.4 4.4 slice-start.3
  525.8 3.8 copy-start.12
  534.8 10.1 copy-start.8
  537.1 7.8 copy-start.10
  538.3 344.3 %reduce-scatter.13.cloned.1.call-start = ((), (), s32[]{:S(2)}) async-start(), calls=%async_computation.10 | async-start | bytes 12976128 | tf_op jit(solution)/shard_map/reduce_scatter | solution.py:303
  557.5 1.0 copy-start.6
  557.5 531.7 %reduce-scatter.11.cloned.1.call-start = ((), (), s32[]{:S(2)}) async-start(), calls=%async_computation.7 | async-start | bytes 17436672 | tf_op jit(solution)/shard_map/reduce_scatter | solution.py:28
  568.9 0.9 copy-start.4
  568.9 778.1 %reduce-scatter.9.cloned.1.call-start = ((), (), s32[]{:S(2)}) async-start(), calls=%async_computation.6 | async-start | bytes 22167552 | tf_op jit(solution)/shard_map/reduce_scatter | solution.py:28
  569.9 2.7 copy-start.13
  605.9 809.4 %all-reduce.10.cloned.1.call-start = ((), (), s32[]{:S(2)}) async-start(), calls=%async_computation.8 | async-start | bytes 3153920 | tf_op jit(solution)/shard_map/psum | solution.py:38
  1350.4 16.7 %copy-start.9 = (bf16[16,64,128]{2,1,0:T(8,128)(2,1)S(1)}, bf16[16,64,128]{2,1,0:T(8,128)(2,1)}, u32[]{:S(2)}) copy-start(bf16[16,64,128]{2,1,0:T(8,128)(2,1)} %copy-done.8) | copy-start | bytes 786436
  1350.4 16.7 %copy-start.11 = (bf16[1,128,16,64]{1,3,2,0:T(8,128)(2,1)S(1)}, bf16[1,128,16,64]{1,3,2,0:T(8,128)(2,1)}, u32[]{:S(2)}) copy-start(bf16[1,128,16,64]{1,3,2,0:T(8,128)(2,1)} %copy-done.10) | copy-start | bytes 786436
  1417.6 3.1 slice-start
  1419.8 2.6 copy-start.7
Sparse Core Ops, SparseCore 0:
  9.7 148.1 all-gather.12
  160.2 169.6 all-gather.10
  332.1 173.5 all-gather.8
  538.4 150.4 reduce-scatter.14
  691.3 191.2 reduce-scatter.12
  885.0 204.1 reduce-scatter.10
  1091.7 255.2 reduce-scatter.8
  1367.2 48.0 all-reduce.9
where the time goes:
time: 1440 us; the launch traced here: 1430 us
  waiting for transfers between devices  979 us (68%)
  blocking collectives  274 us (19%)
  local copies, waits for them, and re-layouts  87.5 us (6%)
  matrix products  58.9 us (4%)
  between operations  17 us (1%)
    reduce_scatter x2, waiting for transfers between devices, in_one_piece(): lax.psum_scatter(both, axis, scatter_dimension=dim, tiled=True)  461 us
    all_gather x2, waiting for transfers between devices, sent_together(): filled, at, done = (lax.all_gather(both, axis, axis=dim, tiled=True), 0, [])  331 us
    unnamed x2, blocking collectives  206 us
    reduce_scatter x1, waiting for transfers between devices, body(): lax.psum_scatter(terms[0], 'shard', scatter_dimension=0, tiled=True)  144 us
    all_gather x1, blocking collectives, body(): lax.all_gather(b_qv[layer_index], 'shard', axis=1, tiled=True)  68.2 us
    psum x1, waiting for transfers between devices, together(): so_far = lax.psum(line, axis)  42.4 us
  transfers between devices with their start and end apart: 8, of which 6 were waited for; matrix products, arithmetic and copies ran while one was open for 7% of the time, Pallas kernels for 0%

commit v1 on v0

--- a/solution.py
+++ b/solution.py
@@ -35,7 +35,7 @@
 
 def together(arrays, axis):
     line, at, done = (jnp.concatenate([a.reshape(-1) for a in arrays]), 0, [])
-    so_far = lax.psum(line, axis)
+    so_far = jnp.sum(lax.all_gather(line, axis), axis=0)
     for a in arrays:
         done.append(so_far[at : at + a.size].reshape(a.shape))
         at += a.size

time: 1440 us -> 1470 us (1.021)
  other arithmetic: 14.2 us -> 44.6 us
    psum x1 -> x0, waiting for transfers between devices: 42.4 us -> none  [together(): so_far = lax.psum(line, axis)]
    all_gather x0 -> x1, waiting for transfers between devices: none -> 41.7 us  [together(): so_far = jnp.sum(lax.all_gather(line, axis), axis=0)]
    reduce_sum x0 -> x1, other arithmetic: none -> 30.4 us  [together(): so_far = jnp.sum(lax.all_gather(line, axis), axis=0)]
    unnamed x70 -> x69, local copies, waits for them, and re-layouts: 20.7 us -> 29.6 us
where the time goes in v1:
time: 1470 us; the launch traced here: 1460 us
  waiting for transfers between devices  978 us (67%)
  blocking collectives  274 us (19%)
  local copies, waits for them, and re-layouts  88.7 us (6%)
  matrix products  58.9 us (4%)
  other arithmetic  44.6 us (3%)
  between operations  16.9 us (1%)
    reduce_scatter x2, waiting for transfers between devices, in_one_piece(): lax.psum_scatter(both, axis, scatter_dimension=dim, tiled=True)  464 us
    all_gather x2, waiting for transfers between devices, sent_together(): filled, at, done = (lax.all_gather(both, axis, axis=dim, tiled=True), 0, [])  330 us
    unnamed x2, blocking collectives  206 us
    reduce_scatter x1, waiting for transfers between devices, body(): lax.psum_scatter(terms[0], 'shard', scatter_dimension=0, tiled=True)  142 us
    all_gather x1, blocking collectives, body(): lax.all_gather(b_qv[layer_index], 'shard', axis=1, tiled=True)  68.2 us
    all_gather x1, waiting for transfers between devices, together(): so_far = jnp.sum(lax.all_gather(line, axis), axis=0)  41.7 us
    reduce_sum x1, other arithmetic, together(): so_far = jnp.sum(lax.all_gather(line, axis), axis=0)  30.4 us
    unnamed x69, local copies, waits for them, and re-layouts  29.6 us
  transfers between devices with their start and end apart: 8, of which 6 were waited for; matrix products, arithmetic and copies ran while one was open for 7% of the time, Pallas kernels for 0%

profile of v1, /device:TPU:1, one launch (start us, length us, event | category | flops | bytes accessed | tf_op | source)
XLA Modules:
  0.0 1461.9 jit_solution(1826189338528841422)
XLA Ops:
  8.8 1.8 pad_maximum_fusion.4
  12.9 2.0 concatenate.21
  17.6 74.4 %all-reduce.7 = (bf16[1024]{0:T(1024)(128)(2,1)S(1)}, bf16[1024]{0:T(1024)(128)(2,1)S(1)}, bf16[1024]{0:T(1024)(128)(2,1)S(1)}) all-reduce(bf16[1024]{0:T(1024)(128)(2,1)S(1)} %dynamic-update-slice, bf16[1024]{0:T(1024)(128)(2,1)S(1)} %dynamic-update-slice.2, ...), channel_id=4, replica_groups=mesh['rep'=4,'shard'=32] {'shard'}, use_global_device_ids=true, to_apply=%add | all-reduce | flops 3072 | bytes 12288
  92.2 68.2 %all-gather.1 = bf16[1,2,1024]{1,0,2:T(2,128)(2,1)S(1)} all-gather(bf16[1,2,32]{1,0,2:T(2,128)(2,1)S(1)} %copy.83), channel_id=3, replica_groups=mesh['rep'=4,'shard'=32] {'shard'}, dimensions={2}, use_global_device_ids=true | all-gather | bytes 4224 | tf_op jit(solution)/shard_map/all_gather | solution.py:255
  161.0 7.2 slice_reduce_fusion
  168.3 3.8 fusion.11
  173.6 156.3 %all-gather.14.cloned.1.call-done = bf16[4096,1025]{1,0:T(8,128)(2,1)} async-done(((bf16[128,1025]{1,0:T(8,128)(2,1)}), bf16[4096,1025]{1,0:T(8,128)(2,1)}) %all-gather.14.cloned.1.call-update) | async-done | bytes 8396816 | tf_op jit(solution)/shard_map/all_gather | solution.py:17
  329.9 1.6 convert_reduce_fusion
  331.5 174.2 %all-gather.12.cloned.1.call-done = bf16[1024,5123]{1,0:T(8,128)(2,1)} async-done(((bf16[32,5123]{1,0:T(8,128)(2,1)}), bf16[1024,5123]{1,0:T(8,128)(2,1)}) %all-gather.12.cloned.1.call-update) | async-done | bytes 10491920 | tf_op jit(solution)/shard_map/all_gather | solution.py:17
  505.7 1.6 convert_reduce_fusion.3
  507.3 2.1 fusion.110
  509.7 6.9 fusion.13
  516.7 3.2 fusion.111
  520.5 1.0 fusion.102
  521.4 4.3 fusion.114
  525.8 3.7 multiply_reduce_fusion.1
  529.8 0.8 fusion.53
  531.3 1.3 fusion.115
  532.7 2.1 convolution_convert_fusion
  534.8 2.3 fusion.106
  537.3 1.0 copy.109
  538.5 6.4 convolution_bitcast_fusion
  544.9 12.6 copy.107
  557.6 1.0 copy-done.6
  558.5 4.0 fusion.91
  562.5 6.4 pad_maximum_fusion
  569.9 2.7 fusion.88
  572.6 8.3 fusion.73
  580.8 25.0 %concatenate.24 = f32[1024,5123]{1,0:T(8,128)} concatenate(f32[1024,1024]{1,0:T(8,128)} %fusion.88, f32[1024,1]{1,0:T(8,128)S(1)} %copy.98, f32[1024,1]{1,0:T(8,128)S(1)} %copy.99, f32[1024,1]{1,0:T(8,128)S(1)} %copy.100, f32[1024,4096]{1,0:T(8,128)} %fusion.73), dimensions={1} | concatenate | bytes 41967616 | tf_op jit(solution)/shard_map/concatenate | solution.py:27
  606.6 131.1 %all-reduce.6 = (f32[1024]{0:T(1024)S(1)}, f32[1024]{0:T(1024)S(1)}, f32[1024]{0:T(1024)S(1)}) all-reduce(f32[1024]{0:T(1024)S(1)} %get-tuple-element.35, f32[1024]{0:T(1024)S(1)} %get-tuple-element.19, f32[1024]{0:T(1024)S(1)} %convert_reduce_fusion.1), channel_id=12, replica_groups=mesh['rep'=4,'shard'=32] {'shard'}, use_global_device_ids=true, to_apply=%region_22.23.clone | all-reduce | flops 3072 | bytes 24576
  739.4 141.9 %reduce-scatter.13.cloned.1.call-done = f32[32,3072]{1,0:T(8,128)} async-done(((f32[1024,3072]{1,0:T(8,128)}), f32[32,3072]{1,0:T(8,128)}) %reduce-scatter.13.cloned.1.call-update) | async-done | bytes 393232 | tf_op jit(solution)/shard_map/reduce_scatter | solution.py:303
  881.3 1.1 copy.111
  882.3 207.8 %reduce-scatter.11.cloned.1.call-done = f32[128,1025]{0,1:T(8,128)} async-done(((f32[4096,1025]{0,1:T(8,128)}), f32[128,1025]{0,1:T(8,128)}) %reduce-scatter.11.cloned.1.call-update) | async-done | bytes 524816 | tf_op jit(solution)/shard_map/reduce_scatter | solution.py:28
  1090.1 1.1 slice.157
  1091.5 1.2 slice_bitcast_fusion.9
  1092.7 255.8 %reduce-scatter.9.cloned.1.call-done = f32[32,5123]{1,0:T(8,128)} async-done(((f32[1024,5123]{1,0:T(8,128)}), f32[32,5123]{1,0:T(8,128)}) %reduce-scatter.9.cloned.1.call-update) | async-done | bytes 655760 | tf_op jit(solution)/shard_map/reduce_scatter | solution.py:28
  1348.5 1.2 slice_bitcast_fusion
  1349.7 0.9 copy.113
  1350.6 0.9 slice_bitcast_fusion.1
  1351.6 1.1 slice_reduce_fusion.2
  1352.7 10.6 concatenate.26
  1363.3 8.1 reshape.331
  1371.4 5.8 fusion.50
  1377.2 41.7 %all-gather.18.cloned.1.call-done = f32[4,1,393600]{2,1,0:T(1,128)} async-done(((f32[1,1,393600]{2,1,0:T(1,128)}), f32[4,1,393600]{2,1,0:T(1,128)}) %all-gather.18.cloned.1.call-update) | async-done | bytes 6297616 | tf_op jit(solution)/shard_map/all_gather | solution.py:38
  1418.9 30.4 %reduce_sum.199 = f32[393600]{0:T(1024)S(1)} reduce(f32[4,1,393600]{2,1,0:T(1,128)} %all-gather.18.cloned.1.call-done, f32[]{:T(128)} %constant.22.clone.1), dimensions={0,1}, to_apply=%region_27.28 | reduce | flops 1180800 | bytes 7872004 | tf_op jit(solution)/shard_map/reduce_sum | solution.py:38
  1452.3 0.9 stack_reshape.19
  1453.2 0.8 stack_reshape.15
  1454.0 0.9 stack_reshape.18
  (128 shorter events, 15.5 us)
Async XLA Ops:
  7.2 8.5 copy-start.16
  7.2 9.7 copy-start.18
  7.2 10.0 copy-start.19
  7.2 10.2 copy-start.20
  7.2 84.9 %copy-start.17 = (bf16[1,2,32]{2,1,0:T(2,128)(2,1)S(1)}, bf16[1,2,32]{2,1,0:T(2,128)(2,1)}, u32[]{:S(2)}) copy-start(bf16[1,2,32]{2,1,0:T(2,128)(2,1)} %param.19) | copy-start | bytes 388
  7.2 161.0 %all-gather.16.cloned.1.call-start = ((), (), s32[]{:S(2)}) async-start(), calls=%async_computation.8 | async-start | bytes 6488064 | tf_op jit(solution)/shard_map/all_gather | solution.py:254
  8.0 321.9 %all-gather.14.cloned.1.call-start = ((), (), s32[]{:S(2)}) async-start(), calls=%async_computation.5 | async-start | bytes 9732096 | tf_op jit(solution)/shard_map/all_gather | solution.py:17
  10.6 157.6 %copy-start = (bf16[1,128,1024]{2,1,0:T(8,128)(2,1)S(1)}, bf16[1,128,1024]{2,1,0:T(8,128)(2,1)}, u32[]{:S(2)}) copy-start(bf16[1,128,1024]{2,1,0:T(8,128)(2,1)} %param.15) | copy-start | bytes 786436
  10.6 495.1 %all-gather.12.cloned.1.call-start = ((), (), s32[]{:S(2)}) async-start(), calls=%async_computation.4 | async-start | bytes 11083776 | tf_op jit(solution)/shard_map/all_gather | solution.py:17
  14.9 723.0 %reduce-scatter.15.cloned.1.call-start = ((), (), s32[]{:S(2)}) async-start(), calls=%async_computation.11 | async-start | bytes 540672
  172.4 1.2 copy-start.14
  172.6 1.1 copy-start.13
  173.6 335.8 %copy-start.3 = (bf16[16,64,128]{2,1,0:T(8,128)(2,1)}, bf16[16,64,128]{2,1,0:T(8,128)(2,1)S(1)}, u32[]{:S(2)}) copy-start(bf16[16,64,128]{2,1,0:T(8,128)(2,1)S(1)} %convolution_convert_fusion.1) | copy-start | bytes 786436
  509.7 7.0 copy-start.15
  516.7 4.8 copy-start.1
  516.7 3.5 copy-start.2
  520.5 5.3 slice-start
  521.4 4.4 copy-start.5
  521.4 4.4 slice-start.1
  521.4 4.4 slice-start.2
  525.8 3.7 copy-start.11
  534.8 10.1 copy-start.7
  537.1 7.8 copy-start.9
  538.3 343.0 %reduce-scatter.13.cloned.1.call-start = ((), (), s32[]{:S(2)}) async-start(), calls=%async_computation.10 | async-start | bytes 12976128 | tf_op jit(solution)/shard_map/reduce_scatter | solution.py:303
  557.5 1.0 copy-start.6
  557.5 532.6 %reduce-scatter.11.cloned.1.call-start = ((), (), s32[]{:S(2)}) async-start(), calls=%async_computation.7 | async-start | bytes 17436672 | tf_op jit(solution)/shard_map/reduce_scatter | solution.py:28
  568.9 0.9 copy-start.4
  569.0 779.5 %reduce-scatter.9.cloned.1.call-start = ((), (), s32[]{:S(2)}) async-start(), calls=%async_computation.6 | async-start | bytes 22167552 | tf_op jit(solution)/shard_map/reduce_scatter | solution.py:28
  569.9 2.7 copy-start.12
  605.9 813.0 %all-gather.18.cloned.1.call-start = ((), (), s32[]{:S(2)}) async-start(), calls=%async_computation.9 | async-start | bytes 7872000 | tf_op jit(solution)/shard_map/all_gather | solution.py:38
  1363.3 8.1 copy-start.8
  1363.3 8.1 copy-start.10
Sparse Core Ops, SparseCore 0:
  9.7 148.1 all-gather.15
  160.2 169.6 all-gather.13
  332.1 173.5 all-gather.11
  538.4 150.4 reduce-scatter.14
  691.3 189.8 reduce-scatter.12
  883.7 206.4 reduce-scatter.10
  1092.7 255.7 reduce-scatter.8
  1371.5 47.3 all-gather.17
